TPU v7x, 256 devices: a whole 4x4x8 slice. The times are simulated.
256 devices in a mesh: rows: 16 (over z, core), cols: 16 (over y, x).
Axes of the slice: x: 4, y: 4, z: 8, core: 2. Of those that a mesh axis runs over, the one named last changes fastest.
Arguments:
- window_slab: float32 [24576, 4096], P('rows', 'cols'), may hold values from -6 to 6
- first_inverse: float32 [2, 512, 512], replicated, may hold values from -2 to 2, as said below
- first_factor: float32 [2, 512, 24576], P(None, 'cols', 'rows'), may hold values from -0.25 to 0.25
- second_inverse: float32 [2, 512, 512], replicated, may hold values from -2 to 2, as said below
- second_factor: float32 [2, 512, 4096], P(None, 'cols', 'rows'), may hold values from -0.25 to 0.25
Outputs:
- reduced: float32 [24576, 4096], P('cols', 'rows')
Inputs may be any that keep to these rules, and one draw needn't show every extreme that they name: first_inverse[k] is lower triangular with diagonal entries from 0.5 to 2. second_inverse[k] is lower triangular with diagonal entries from 0.5 to 2.
All inputs are finite; a program needn't handle non-finite values.
Results may differ from a plain program's by a relative error of at most 0.0001.
Values sent between devices are 32-bit elements; how exact they have to be, the bound alone decides.
A program may use at most 64 MiB of HBM per device.

v0:
```python
import jax
import jax.numpy as jnp
from jax import lax
from jax.sharding import PartitionSpec as P

BLOCK = 128


HIGHEST = lax.Precision.HIGHEST
CONTRACT_ROWS = (((0,), (0,)), ((), ()))
CONTRACT_COLS = (((1,), (1,)), ((), ()))


def right_solve(current, first_column, inverses, total_of, update_of):
    height, breadth = current.shape
    panel_count = inverses.shape[0]
    panel_width = inverses.shape[1]
    portion = min(breadth, panel_width)
    columns = first_column + lax.broadcasted_iota(jnp.int32, (1, breadth), 1)
    for panel_index in range(panel_count):
        panel_start = panel_index * panel_width
        panel_end = panel_start + panel_width
        inner_offset = jnp.clip(first_column - panel_start, 0, panel_width - portion)
        member = jnp.logical_and(first_column < panel_end, first_column + breadth > panel_start)
        own_columns = current
        inverse_cols = lax.dynamic_slice_in_dim(inverses[panel_index], inner_offset, portion, 1)
        partial_value = lax.dot_general(
            own_columns,
            inverse_cols,
            CONTRACT_COLS,
            precision=HIGHEST,
            preferred_element_type=jnp.float32,
        )
        solved = total_of(jnp.where(member, partial_value, 0.0))
        update = update_of(panel_index, solved)
        current = jnp.where(columns >= panel_end, current - update, current)
        mine_cols = lax.dynamic_slice_in_dim(solved, inner_offset, portion, 1)
        present = current
        current = jnp.where(member, mine_cols, present)
    return current


def on_device(window_slab, first_inverse, first_factor, second_inverse, second_factor):
    row_count = lax.axis_size("rows")
    row_index = lax.axis_index("rows")
    row_share, breadth = window_slab.shape
    panel_count = first_inverse.shape[0]
    panel_width = first_inverse.shape[1]
    blocks_per_panel = panel_width // BLOCK
    local_rows = lax.broadcasted_iota(jnp.int32, (row_share, 1), 0)
    logical_rows = (local_rows // BLOCK * row_count + row_index) * BLOCK + local_rows % BLOCK
    current = window_slab
    for panel_index in range(panel_count):
        panel_start = panel_index * panel_width
        panel_end = panel_start + panel_width
        local_block = panel_start // (row_count * BLOCK)
        first_group = panel_start // BLOCK % row_count
        member = jnp.logical_and(
            row_index >= first_group, row_index < first_group + blocks_per_panel
        )
        offset = jnp.clip(row_index - first_group, 0, blocks_per_panel - 1) * BLOCK
        own_rows = current[local_block * BLOCK : (local_block + 1) * BLOCK]
        inverse_cols = lax.dynamic_slice_in_dim(first_inverse[panel_index], offset, BLOCK, 1)
        partial_value = jnp.dot(
            inverse_cols, own_rows, precision=HIGHEST, preferred_element_type=jnp.float32
        )
        solved = lax.psum(jnp.where(member, partial_value, 0.0), "rows")
        update = lax.dot_general(
            lax.all_gather(first_factor[panel_index], "cols", axis=0, tiled=True),
            solved,
            CONTRACT_ROWS,
            precision=HIGHEST,
            preferred_element_type=jnp.float32,
        )
        current = jnp.where(logical_rows >= panel_end, current - update, current)
        mine_rows = lax.dynamic_slice_in_dim(solved, offset, BLOCK, 0)
        present = current[local_block * BLOCK : (local_block + 1) * BLOCK]
        current = lax.dynamic_update_slice_in_dim(
            current, jnp.where(member, mine_rows, present), local_block * BLOCK, 0
        )
    turned = lax.all_to_all(
        lax.all_to_all(current, "cols", split_axis=0, concat_axis=1, tiled=True),
        "rows",
        split_axis=1,
        concat_axis=0,
        tiled=True,
    )
    height, narrow = turned.shape

    def total_rows(partial_sum):
        return lax.psum(partial_sum, "rows")

    def update_rows(panel_number, solved_cols):
        return jnp.dot(
            solved_cols,
            lax.all_gather(second_factor[panel_number], "cols", axis=0, tiled=True),
            precision=HIGHEST,
            preferred_element_type=jnp.float32,
        )

    reduced = right_solve(turned, row_index * narrow, second_inverse, total_rows, update_rows)
    return reduced


def solution(mesh):
    return jax.shard_map(
        on_device,
        mesh=mesh,
        in_specs=(P("rows", "cols"), P(), P(None, "cols", "rows"), P(), P(None, "cols", "rows")),
        out_specs=P("cols", "rows"),
        check_vma=False,
    )
```

profile of v0, /device:TPU:1, one launch (start us, length us, event | category | flops | bytes accessed | tf_op | source)
XLA Modules:
  0.0 586.9 jit_solution(826307015627052051)
XLA Ops:
  7.4 0.0 all-reduce.5.cloned.1.call-start
  7.4 0.0 copy-start.1
  7.4 2.8 fusion.57
  10.2 0.0 copy-start.2
  10.2 0.0 copy-done.1
  10.2 1.4 convolution_select_fusion.3
  11.5 0.0 all-reduce.5.cloned.1.call-update
  11.6 0.0 all-gather.7.cloned.1.call-start
  11.6 0.0 copy-done.2
  11.6 0.8 fusion.58
  12.4 0.0 all-gather.7.cloned.1.call-update
  12.4 0.0 all-gather.9.cloned.1.call-start
  12.5 0.5 all-gather.9.cloned.1.call-update
  13.0 0.0 all-reduce.7.cloned.1.call-start
  13.1 113.7 %all-reduce.5.cloned.1.call-done = f32[512,256]{1,0:T(8,128)} async-done(((f32[512,256]{1,0:T(8,128)}), f32[512,256]{1,0:T(8,128)}) %all-reduce.5.cloned.1.call-update) | async-done | bytes 524304 | tf_op jit(solution)/shard_map/psum | solution.py:67
  126.8 0.0 all-gather.7.cloned.1.call-done
  126.8 7.2 %fusion.14 = f32[1536,256]{1,0:T(8,128)S(1)} fusion(f32[1536,256]{1,0:T(8,128)S(1)} %copy-done.1, f32[512,256]{1,0:T(8,128)} %all-reduce.5.cloned.1.call-done, f32[1,512,1536]{2,1,0:T(8,128)} %all-gather.7.cloned.1.call-done, pred[1536]{0:T(1024)(128)(4,1)S(1)} %broadcast_compare_fusion), kind=kOutput, calls=%fused_computation.14 | convolution fusion | flops 2416705536 | bytes 6817280 | tf_op jit(solution)/shard_map/dot_general | solution.py:68
  134.0 2.4 convolution_select_fusion.2
  136.4 0.0 all-reduce.7.cloned.1.call-update
  136.5 0.9 fusion.38
  137.4 0.0 all-gather.9.cloned.1.call-done
  137.4 108.6 %all-reduce.7.cloned.1.call-done = f32[512,256]{1,0:T(8,128)} async-done(((f32[512,256]{1,0:T(8,128)}), f32[512,256]{1,0:T(8,128)}) %all-reduce.7.cloned.1.call-update) | async-done | bytes 524304 | tf_op jit(solution)/shard_map/psum | solution.py:67
  246.1 7.5 %fusion.23 = f32[1536,256]{1,0:T(8,128)S(1)} fusion(f32[1536,256]{1,0:T(8,128)S(1)} %fusion.38, f32[512,256]{1,0:T(8,128)} %all-reduce.7.cloned.1.call-done, f32[1,512,1536]{2,1,0:T(8,128)} %all-gather.9.cloned.1.call-done, pred[1536]{0:T(1024)(128)(4,1)S(1)} %broadcast_compare_fusion.1), kind=kOutput, calls=%fused_computation.17 | convolution fusion | flops 2416705536 | bytes 6817280 | tf_op jit(solution)/shard_map/dot_general | solution.py:68
  253.5 0.9 fusion.36
  254.5 28.3 %all_to_all.32 = f32[16,96,256]{2,1,0:T(8,128)} all-to-all(f32[16,96,256]{2,1,0:T(8,128)S(1)} %bitcast.61), channel_id=1, replica_groups=mesh['rows'=16,'cols'=16] {'cols'}, dimensions={0} | all-to-all | bytes 3145728 | tf_op jit(solution)/shard_map/all_to_all | solution.py:82
  282.8 6.9 %all-to-all-start.1 = ((f32[96,16,256]{2,0,1:T(8,128)}), f32[96,16,256]{2,0,1:T(8,128)S(1)}, u32[]{:S(2)}, u32[]{:S(2)}) async-start(f32[96,16,256]{2,0,1:T(8,128)} %bitcast.7), calls=%async_computation.1 | async-start | bytes 3145728 | tf_op jit(solution)/shard_map/all_to_all | solution.py:81
  289.7 0.2 all-reduce.9.cloned.1.call-start
  289.9 2.7 fusion.56
  292.6 35.5 %all-to-all-done.1 = f32[96,16,256]{2,0,1:T(8,128)S(1)} async-done(((f32[96,16,256]{2,0,1:T(8,128)}), f32[96,16,256]{2,0,1:T(8,128)S(1)}, u32[]{:S(2)}, u32[]{:S(2)}) %all-to-all-start.1) | async-done | bytes 1572896 | tf_op jit(solution)/shard_map/all_to_all | solution.py:81
  328.1 4.5 convolution_select_fusion.1
  332.6 0.0 copy-start.3
  332.6 0.0 all-reduce.9.cloned.1.call-update
  332.7 0.0 all-reduce.11.cloned.1.call-start
  332.7 0.7 copy-done.3
  333.5 19.8 %all-gather.2 = f32[1,512,256]{2,1,0:T(8,128)} all-gather(f32[1,32,256]{2,1,0:T(8,128)S(1)} %get-tuple-element.12), channel_id=4, replica_groups=mesh['rows'=16,'cols'=16] {'cols'}, dimensions={1}, use_global_device_ids=true | all-gather | bytes 557056 | tf_op jit(solution)/shard_map/all_gather | solution.py:96
  353.2 91.8 %all-reduce.9.cloned.1.call-done = f32[1536,512]{1,0:T(8,128)} async-done(((f32[1536,512]{1,0:T(8,128)}), f32[1536,512]{1,0:T(8,128)}) %all-reduce.9.cloned.1.call-update) | async-done | bytes 3145744 | tf_op jit(solution)/shard_map/psum | solution.py:91
  445.1 0.0 copy-start
  445.1 5.3 fusion.7
  450.3 0.0 copy-done
  450.3 4.5 convolution_select_fusion
  454.8 0.0 all-reduce.11.cloned.1.call-update
  454.9 19.2 %all-gather.3 = f32[1,512,256]{2,1,0:T(8,128)S(1)} all-gather(f32[1,32,256]{2,1,0:T(8,128)S(1)} %get-tuple-element.11), channel_id=5, replica_groups=mesh['rows'=16,'cols'=16] {'cols'}, dimensions={1}, use_global_device_ids=true | all-gather | bytes 557056 | tf_op jit(solution)/shard_map/all_gather | solution.py:96
  474.1 99.3 %all-reduce.11.cloned.1.call-done = f32[1536,512]{1,0:T(8,128)} async-done(((f32[1536,512]{1,0:T(8,128)}), f32[1536,512]{1,0:T(8,128)}) %all-reduce.11.cloned.1.call-update) | async-done | bytes 3145744 | tf_op jit(solution)/shard_map/psum | solution.py:91
  573.4 6.4 %fusion.5 = f32[1536,256]{1,0:T(8,128)} fusion(f32[1536,256]{1,0:T(8,128)S(1)} %fusion.7, f32[1536,512]{1,0:T(8,128)} %all-reduce.11.cloned.1.call-done, s32[]{:T(128)S(6)} %min.16, pred[256]{0:T(512)(128)(4,1)S(1)} %fusion.54, pred[]{:T(512)S(6)} %and.52, f32[1,512,256]{2,1,0:T(8,128)S(1)} %all-gather.3), kind=kOutput, calls=%fused_computation.8 | convolution fusion | flops 2417098752 | bytes 8388869 | tf_op jit(solution)/shard_map/dot_general | solution.py:94
  (5 shorter events, 0.0 us)
Async XLA Ops:
  7.4 119.4 %all-reduce.5.cloned.1.call-start = ((), (), s32[]{:S(2)}) async-start(), calls=%async_computation.2 | async-start | bytes 1048576 | tf_op jit(solution)/shard_map/psum | solution.py:67
  7.4 2.8 copy-start.1
  10.2 1.4 copy-start.2
  11.6 115.2 %all-gather.7.cloned.1.call-start = ((), (), s32[]{:S(2)}) async-start(), calls=%async_computation.6 | async-start | bytes 3342336 | tf_op jit(solution)/shard_map/all_gather | solution.py:69
  12.4 125.0 %all-gather.9.cloned.1.call-start = ((), (), s32[]{:S(2)}) async-start(), calls=%async_computation.7 | async-start | bytes 3342336 | tf_op jit(solution)/shard_map/all_gather | solution.py:69
  13.0 233.1 %all-reduce.7.cloned.1.call-start = ((), (), s32[]{:S(2)}) async-start(), calls=%async_computation.3 | async-start | bytes 1048576 | tf_op jit(solution)/shard_map/psum | solution.py:67
  282.8 45.4 %all-to-all-start.1 = ((f32[96,16,256]{2,0,1:T(8,128)}), f32[96,16,256]{2,0,1:T(8,128)S(1)}, u32[]{:S(2)}, u32[]{:S(2)}) async-start(f32[96,16,256]{2,0,1:T(8,128)} %bitcast.7), calls=%async_computation.1 | async-start | bytes 3145728 | tf_op jit(solution)/shard_map/all_to_all | solution.py:81
  289.7 155.4 %all-reduce.9.cloned.1.call-start = ((), (), s32[]{:S(2)}) async-start(), calls=%async_computation.4 | async-start | bytes 6291456 | tf_op jit(solution)/shard_map/psum | solution.py:91
  332.6 0.8 copy-start.3
  332.7 240.7 %all-reduce.11.cloned.1.call-start = ((), (), s32[]{:S(2)}) async-start(), calls=%async_computation.5 | async-start | bytes 6291456 | tf_op jit(solution)/shard_map/psum | solution.py:91
  445.1 5.3 copy-start
Sparse Core Ops, SparseCore 0:
  11.7 115.0 all-reduce.4
  136.6 109.4 all-reduce.6
  332.8 112.2 all-reduce.8
  455.0 118.3 all-reduce.10
Sparse Core Ops, SparseCore 1:
  14.8 56.3 all-gather.6
  73.4 51.8 all-gather.8
where the time goes:
time: 587 us
  waiting for transfers between devices  450 us (77%)
  blocking collectives  67.2 us (11%)
  matrix products  39.2 us (7%)
  between operations  14.7 us (3%)
  starting transfers between devices  7.32 us (1%)
  local copies, waits for them, and re-layouts  7.02 us (1%)
    psum x2, waiting for transfers between devices, on_device(): solved = lax.psum(jnp.where(member, partial_value, 0.0), 'rows')  222 us
    psum x2, waiting for transfers between devices, total_rows(): return lax.psum(partial_sum, 'rows')  191 us
    all_gather x2, blocking collectives, update_rows(): lax.all_gather(second_factor[panel_number], 'cols', axis=0, tiled=True)  38.9 us
    all_to_all x1, waiting for transfers between devices, on_device(): lax.all_to_all(lax.all_to_all(current, 'cols', split_axis=0, concat_axis=...  35.5 us
    all_to_all x1, blocking collectives, on_device(): lax.all_to_all(current, 'cols', split_axis=0, concat_axis=1, tiled=True)  28.3 us
    dot_general x2, matrix products, on_device(): lax.dot_general(lax.all_gather(first_factor[panel_index], 'cols', axis=0,...  14.7 us
  transfers between devices with their start and end apart: 7, of which 5 were waited for; matrix products, arithmetic and copies ran while one was open for 2% of the time, Pallas kernels for 0%

commit v1 on v0

v1 whole, which is shorter than its diff:
```python
import jax
import jax.numpy as jnp
from jax import lax
from jax.experimental import pallas as pl
from jax.experimental.pallas import tpu as pltpu
from jax.sharding import PartitionSpec as P

MESH = pl.DeviceIdType.MESH
F32 = jnp.float32
BF16 = jnp.bfloat16
NN = (((1,), (0,)), ((), ()))
NT = (((1,), (1,)), ((), ()))


def split(value):
    high = value.astype(BF16)
    return high, (value - high.astype(F32)).astype(BF16)


def product(a, b, dims=NN):
    def dot(u, v):
        return lax.dot_general(u, v, dims, preferred_element_type=F32)

    return dot(a[0], b[0]) + (dot(a[0], b[1]) + dot(a[1], b[0]))


def remote(src, dst, send_sem, recv_sem, device):
    return pltpu.make_async_remote_copy(
        src_ref=src,
        dst_ref=dst,
        send_sem=send_sem,
        recv_sem=recv_sem,
        device_id=device,
        device_id_type=MESH,
    )


class Gather4:
    def __init__(self, index, device, slot, half, send, recv):
        self.up, self.down, self.far = (index + 1) % 4, (index + 3) % 4, (index + 2) % 4
        self.slot = slot
        to_up, to_down = device(self.up), device(self.down)
        own = slot(index)
        self.first = [
            remote(own, own, send.at[0], recv.at[0], to_up),
            remote(own, own, send.at[1], recv.at[1], to_down),
        ]
        self.second = [
            remote(half(0, self.down), half(0, self.down), send.at[2], recv.at[2], to_up),
            remote(half(1, self.up), half(1, self.up), send.at[3], recv.at[3], to_down),
        ]
        self.landing = [
            remote(own, slot(self.down), send.at[0], recv.at[0], to_up),
            remote(own, slot(self.up), send.at[1], recv.at[1], to_down),
            remote(half(0, self.far), half(0, self.far), send.at[2], recv.at[2], to_up),
            remote(half(1, self.far), half(1, self.far), send.at[3], recv.at[3], to_down),
        ]

    def start(self):
        for copy in self.first:
            copy.start()

    def forward(self, then=None):
        for way in (0, 1):
            self.landing[way].wait_recv()
            self.second[way].start()
            if then is not None:
                then(way, (self.down, self.up)[way])

    def finish(self, then=None):
        self.landing[2].wait_recv()
        self.landing[3].wait_recv()
        if then is not None:
            then(2, self.far)

    def drain(self):
        for copy in self.first + self.second:
            copy.wait_send()


class Ring8:
    def __init__(self, z, step, device, is_source, block, send, recv, then=None):
        self.z, self.step_by, self.is_source = z, step, is_source
        self.block, self.send, self.recv, self.then = block, send, recv, then
        self.following = device((z + 8 + step) % 8)

    def copy(self, source, src=None):
        block = self.block(source)
        return remote(
            block if src is None else src,
            block,
            self.send.at[source],
            self.recv.at[source],
            self.following,
        )

    def begin(self, src=None):
        @pl.when(self.is_source(self.z))
        def _():
            self.copy(self.z, src).start()

    def hop(self, count):
        source = (self.z + 16 - self.step_by * count) % 8

        @pl.when(self.is_source(source))
        def _():
            self.copy(source).wait_recv()
            if count < 7:
                self.copy(source).start()
            if self.then is not None:
                self.then(source)

    def drain(self):
        for count in range(7):
            source = (self.z + 16 - self.step_by * count) % 8

            @pl.when(self.is_source(source))
            def _():
                self.copy(source).wait_send()


def kernel(
    slab,
    inverse1,
    factor1,
    inverse2,
    factor2,
    out,
    i1,
    i2,
    xt,
    xp,
    fx,
    gx,
    ft,
    wh,
    wl,
    sb,
    sh,
    sl,
    gt,
    pb,
    zf,
    zh,
    zl,
    db,
    local,
    xp_send,
    xp_recv,
    xs_send,
    xs_recv,
    fz_send,
    fz_recv,
    gz_send,
    gz_recv,
    fxx_send,
    fxx_recv,
    fxy_send,
    fxy_recv,
    gxx_send,
    gxx_recv,
    gxy_send,
    gxy_recv,
    sib_send,
    sib_recv,
    fa_send,
    fa_recv,
    ft_send,
    ft_recv,
    xa_send,
    xa_recv,
    ga_send,
    ga_recv,
    gr_send,
    gr_recv,
    gy_send,
    gy_recv,
    gs_send,
    gs_recv,
    s_send,
    s_recv,
    ss_send,
    ss_recv,
    p_send,
    p_recv,
    o_send,
    o_recv,
):
    r = lax.axis_index("rows")
    c = lax.axis_index("cols")
    z, k = r // 2, r % 2
    y, x = c // 4, c % 4
    way = 1 - 2 * k
    sibling = (2 * z + 1 - k, c)

    def along_y(index):
        return (r, 4 * index + x)

    def along_x(index):
        return (r, 4 * y + index)

    def along_z(index):
        return (2 * index + k, c)

    panel_rows = slab.at[pl.ds(0, 128), :]

    def xp_block(source):
        return xp.at[2 * source + k]

    def xp_to_sibling(source, src=None):
        block = xp_block(source)
        return remote(
            block if src is None else src, block, xs_send.at[source], xs_recv.at[source], sibling
        )

    def in_panels(source):
        return source < 4

    panels = Ring8(
        z,
        way,
        along_z,
        in_panels,
        xp_block,
        xp_send,
        xp_recv,
        then=lambda source: xp_to_sibling(source).start(),
    )
    panels.begin(panel_rows)

    def own_panel():
        return pltpu.make_async_copy(panel_rows, xp_block(z), local.at[0])

    @pl.when(in_panels(z))
    def _():
        xp_to_sibling(z, panel_rows).start()
        own_panel().start()

    fz_src = factor1.at[0, :, pl.ds(0, 128)]
    gz_src = factor2.at[0]

    def fz_dst(which):
        return fx.at[k, which, y, x]

    gz_dst = gx.at[k, y, x]
    fz_own = pltpu.make_async_copy(fz_src, fz_dst((z + 6) % 2), local.at[1])
    gz_own = pltpu.make_async_copy(gz_src, gz_dst, local.at[2])
    f_source = jnp.logical_or(z == 2, z == 3)

    def fz_copy(distance):
        return remote(
            fz_src,
            fz_dst(z % 2),
            fz_send.at[distance - 1],
            fz_recv.at[z % 2],
            along_z((z + distance) % 8),
        )

    def gz_copy(distance):
        return remote(
            gz_src, gz_dst, gz_send.at[distance - 1], gz_recv.at[0], along_z((z + distance) % 8)
        )

    @pl.when(f_source)
    def _():
        fz_own.start()
        for distance in range(1, 8):
            fz_copy(distance).start()

    @pl.when(z == 1)
    def _():
        gz_own.start()
        for distance in range(1, 8):
            gz_copy(distance).start()

    def fa_copy(distance):
        to = (y + distance) % 4
        columns = pl.ds(pl.multiple_of(to * 384, 128), 384)
        return remote(
            factor1.at[:, :, columns],
            ft.at[:, y, x],
            fa_send.at[distance - 1],
            fa_recv.at[distance - 1],
            along_y(to),
        )

    fa_own = pltpu.make_async_copy(
        factor1.at[:, :, pl.ds(pl.multiple_of(y * 384, 128), 384)], ft.at[:, y, x], local.at[3]
    )
    fa_own.start()
    for distance in (1, 3, 2):
        fa_copy(distance).start()

    def xa_copy(distance):
        to = (y + distance) % 4
        return remote(
            slab.at[pl.ds(pl.multiple_of(to * 384, 128), 384), :],
            xt.at[y],
            xa_send.at[distance - 1],
            xa_recv.at[distance - 1],
            along_y(to),
        )

    xa_own = pltpu.make_async_copy(
        slab.at[pl.ds(pl.multiple_of(y * 384, 128), 384), :], xt.at[y], local.at[4]
    )
    xa_own.start()
    for distance in (1, 3, 2):
        xa_copy(distance).start()

    load1 = pltpu.make_async_copy(inverse1, i1, local.at[5])
    load2 = pltpu.make_async_copy(inverse2, i2, local.at[6])
    load1.start()
    load2.start()

    g_plane = r % 4
    g_block = r // 4

    def ga_copy(panel):
        return remote(
            factor2.at[panel],
            gt.at[g_block - 1, panel, y, x],
            ga_send.at[panel],
            ga_recv.at[x, k],
            (2 * z + panel, 4 * y + g_plane),
        )

    def ga_own(panel):
        return pltpu.make_async_copy(
            factor2.at[panel], gt.at[g_block - 1, panel, y, x], local.at[7]
        )

    def ga_stays(panel):
        return jnp.logical_and(g_plane == x, k == panel)

    for panel in (0, 1):

        @pl.when(jnp.logical_and(z >= 2, ga_stays(panel)))
        def _():
            ga_own(panel).start()

        @pl.when(jnp.logical_and(z >= 2, jnp.logical_not(ga_stays(panel))))
        def _():
            ga_copy(panel).start()

    def g_source(source):
        return jnp.logical_and(source >= 2, source % 2 == x // 2)

    g_ring = Ring8(
        z,
        way,
        along_z,
        g_source,
        lambda source: gt.at[source // 2 - 1, k, y],
        gr_send,
        gr_recv,
    )

    def g_slot(index):
        return gt.at[:, k, index]

    def g_to_sibling(number, index):
        return remote(g_slot(index), g_slot(index), gs_send.at[number], gs_recv.at[number], sibling)

    def g_from_sibling(number, index):
        theirs = gt.at[:, 1 - k, index]
        return remote(theirs, theirs, gs_send.at[number], gs_recv.at[number], sibling)

    g_gather = Gather4(
        y,
        along_y,
        g_slot,
        lambda part, index: gt.at[:, k, index, pl.ds(2 * part, 2)],
        gy_send,
        gy_recv,
    )

    fxx = Gather4(
        x,
        along_x,
        lambda index: fx.at[k, :, y, index],
        lambda part, index: fx.at[k, part, y, index],
        fxx_send,
        fxx_recv,
    )
    fxy = Gather4(
        y,
        along_y,
        lambda index: fx.at[k, :, index],
        lambda part, index: fx.at[k, part, index],
        fxy_send,
        fxy_recv,
    )
    gxx = Gather4(
        x,
        along_x,
        lambda index: gx.at[k, y, index],
        lambda part, index: gx.at[k, y, index, pl.ds(16 * part, 16)],
        gxx_send,
        gxx_recv,
    )
    gxy = Gather4(
        y,
        along_y,
        lambda index: gx.at[k, index],
        lambda part, index: gx.at[k, index, pl.ds(2 * part, 2)],
        gxy_send,
        gxy_recv,
    )
    fx_to_sibling = remote(fx.at[k], fx.at[k], sib_send.at[0], sib_recv.at[0], sibling)
    gx_to_sibling = remote(gx.at[k], gx.at[k], sib_send.at[1], sib_recv.at[1], sibling)
    fx_from_sibling = remote(fx.at[1 - k], fx.at[1 - k], sib_send.at[0], sib_recv.at[0], sibling)
    gx_from_sibling = remote(gx.at[1 - k], gx.at[1 - k], sib_send.at[1], sib_recv.at[1], sibling)

    for which in (0, 1):

        @pl.when(z == 2 + which)
        def _():
            fz_own.wait()

        @pl.when(z != 2 + which)
        def _():
            remote(
                fz_src, fz_dst(which), fz_send.at[0], fz_recv.at[which], sibling
            ).wait_recv()

    @pl.when(z == 1)
    def _():
        gz_own.wait()

    @pl.when(z != 1)
    def _():
        remote(gz_src, gz_dst, gz_send.at[0], gz_recv.at[0], sibling).wait_recv()

    fxx.start()
    gxx.start()
    panels.hop(1)
    fxx.forward()
    gxx.forward()
    panels.hop(2)
    fxx.finish()
    fxy.start()
    gxx.finish()
    gxy.start()
    panels.hop(3)
    fxy.forward()
    gxy.forward()
    panels.hop(4)
    fxy.finish()
    fx_to_sibling.start()
    gxy.finish()
    gx_to_sibling.start()
    panels.hop(5)

    f_gather = Gather4(
        x,
        along_x,
        lambda index: ft.at[:, :, index],
        lambda part, index: ft.at[part, :, index],
        ft_send,
        ft_recv,
    )
    fa_own.wait()
    for distance in (1, 3, 2):
        remote(
            ft.at[:, y, x],
            ft.at[:, (y + 4 - distance) % 4, x],
            fa_send.at[distance - 1],
            fa_recv.at[distance - 1],
            sibling,
        ).wait_recv()
    f_gather.start()
    panels.hop(6)

    @pl.when(g_source(z))
    def _():
        for source_x in range(4):
            stays = jnp.logical_and(source_x == x, k == x % 2)
            block = gt.at[z // 2 - 1, k, y, source_x]

            @pl.when(stays)
            def _():
                pltpu.make_async_copy(factor2.at[k], block, local.at[7]).wait()

            @pl.when(jnp.logical_not(stays))
            def _():
                remote(
                    block, block, ga_send.at[0], ga_recv.at[source_x, x % 2], sibling
                ).wait_recv()

    g_ring.begin()
    panels.hop(7)
    f_gather.forward()

    @pl.when(in_panels(z))
    def _():
        own_panel().wait()

    for source in range(4):
        block = xp.at[2 * source + 1 - k]
        remote(block, block, xs_send.at[source], xs_recv.at[source], sibling).wait_recv()
    load1.wait()

    s_gather = Gather4(
        y,
        along_y,
        lambda index: sb.at[index, k],
        lambda part, index: sb.at[index, k, pl.ds(256 * part, 256)],
        s_send,
        s_recv,
    )

    def s_to_sibling(number, index):
        block = sb.at[index, k]
        return remote(block, block, ss_send.at[number], ss_recv.at[number], sibling)

    def s_from_sibling(number, index):
        block = sb.at[index, 1 - k]
        return remote(block, block, ss_send.at[number], ss_recv.at[number], sibling)

    raw0 = split(xp[pl.ds(0, 4)].reshape(512, 256))
    solved0 = product(split(i1[0]), raw0)
    sb[y, 0] = solved0
    sh[...], sl[...] = split(solved0)

    @pl.when(k == 0)
    def _():
        s_gather.start()

    g_ring.hop(1)
    fx_from_sibling.wait_recv()
    remaining = []
    for number in range(4):
        coupling = split(fx[number % 2, number // 2].reshape(512, 128).T)
        remaining.append(xp[4 + number] - product(coupling, (sh[...], sl[...])))
    solved1 = product(split(i1[1]), split(jnp.concatenate(remaining, axis=0)))
    sb[y, 1] = solved1

    @pl.when(k == 1)
    def _():
        s_gather.start()

    f_gather.finish()
    for panel in (0, 1):
        for part in range(4):
            high, rest = split(ft[panel, part].reshape(128, 384).T)
            at = (4 * panel + part) * 128
            wh[:, at : at + 128] = high
            wl[:, at : at + 128] = rest
    g_ring.hop(2)
    s_gather.forward(then=lambda number, index: s_to_sibling(number, index).start())
    g_ring.hop(3)
    g_ring.hop(4)
    s_gather.finish(then=lambda number, index: s_to_sibling(number, index).start())
    g_ring.hop(5)
    xa_own.wait()
    for distance in (1, 3, 2):
        remote(
            xt.at[y],
            xt.at[(y + 4 - distance) % 4],
            xa_send.at[distance - 1],
            xa_recv.at[distance - 1],
            sibling,
        ).wait_recv()
    for number, index in ((0, s_gather.down), (1, s_gather.up), (2, s_gather.far)):
        s_from_sibling(number, index).wait_recv()

    has_panel_rows = jnp.logical_and(y == 0, r < 8)
    own_rows = pl.ds(pl.multiple_of((r % 4) * 128, 128), 128)
    own_panel_index = (r // 4) % 2

    def left(block):
        solved = split(sb[block].reshape(1024, 256))
        return xt[block] - product((wh[...], wl[...]), solved)

    pb[x] = left(0)

    @pl.when(has_panel_rows)
    def _():
        pb[x, pl.ds(0, 128)] = sb[0, own_panel_index, own_rows]

    p_gather = Gather4(
        x,
        along_x,
        lambda index: pb.at[index],
        lambda part, index: pb.at[index, pl.ds(192 * part, 192)],
        p_send,
        p_recv,
    )
    p_gather.start()
    g_ring.hop(6)
    g_ring.hop(7)
    g_gather.start()
    g_to_sibling(3, y).start()

    @pl.loop(1, 4)
    def _(block):
        db[block - 1] = left(block)

        @pl.when(has_panel_rows)
        def _():
            db[block - 1, pl.ds(0, 128)] = sb[block, own_panel_index, own_rows]

    p_gather.forward()
    g_gather.forward(then=lambda number, index: g_to_sibling(number, index).start())
    p_gather.finish()

    load2.wait()
    gx_from_sibling.wait_recv()

    def solve_columns(panel, first):
        total = None
        for part in (0, 1):
            term = product(
                first(part), split(i2[panel, :, 256 * part : 256 * part + 256]), NT
            )
            total = term if total is None else total + term
        for part in (0, 1):
            value = total[:, 256 * part : 256 * part + 256]
            zf[2 * panel + part] = value
            at = 512 * panel + 256 * part
            zh[:, at : at + 256], zl[:, at : at + 256] = split(value)

    def out_copy(block, piece, src):
        return remote(
            src,
            out.at[pl.ds(pl.multiple_of(r * 96, 96), 96), :],
            o_send.at[block, piece],
            o_recv.at[r],
            (4 * block + x, 4 * y + piece),
        )

    def out_own(src):
        return pltpu.make_async_copy(
            src, out.at[pl.ds(pl.multiple_of(r * 96, 96), 96), :], local.at[8]
        )

    def for_pieces(block, values, remote_do, local_do):
        for piece in range(4):
            src = values.at[pl.ds(96 * piece, 96)]
            stays = jnp.logical_and(4 * block + x == r, x == piece)

            @pl.when(stays)
            def _():
                local_do(out_own(src))

            @pl.when(jnp.logical_not(stays))
            def _():
                remote_do(out_copy(block, piece, src))

    def start(copy):
        copy.start()

    solve_columns(0, lambda part: split(pb[part]))
    g_gather.finish(then=lambda number, index: g_to_sibling(number, index).start())
    solved_cols = (zh[:, :512], zl[:, :512])
    remaining = []
    for part in (0, 1):
        coupling = split(gx[part].reshape(512, 256))
        remaining.append(split(pb[2 + part] - product(solved_cols, coupling)))
    solve_columns(1, lambda part: remaining[part])
    for_pieces(0, zf.at[x], start, start)

    for number, index in ((0, g_gather.down), (1, g_gather.up), (2, g_gather.far)):
        g_from_sibling(number, index).wait_recv()
    g_from_sibling(3, y).wait_recv()
    for block in range(1, 4):
        factor = split(gt[block - 1].reshape(1024, 256))
        db[block - 1] = db[block - 1] - product((zh[...], zl[...]), factor)
        for_pieces(block, db.at[block - 1], start, start)

    for source in range(16):
        stays = jnp.logical_and(source == r, x == r % 4)
        rows = out.at[pl.ds(96 * source, 96), :]

        @pl.when(jnp.logical_not(stays))
        def _():
            remote(rows, rows, o_send.at[0, 0], o_recv.at[source], sibling).wait_recv()

    for block in range(4):
        for_pieces(
            block,
            zf.at[x] if block == 0 else db.at[block - 1],
            lambda copy: copy.wait_send(),
            lambda copy: copy.wait(),
        )
    panels.drain()
    g_ring.drain()

    @pl.when(in_panels(z))
    def _():
        xp_to_sibling(z).wait_send()

    for count in range(1, 8):
        source = (z + 16 - way * count) % 8

        @pl.when(in_panels(source))
        def _():
            xp_to_sibling(source).wait_send()

    @pl.when(f_source)
    def _():
        for distance in range(1, 8):
            fz_copy(distance).wait_send()

    @pl.when(z == 1)
    def _():
        for distance in range(1, 8):
            gz_copy(distance).wait_send()

    for distance in (1, 2, 3):
        fa_copy(distance).wait_send()
        xa_copy(distance).wait_send()
    for panel in (0, 1):

        @pl.when(jnp.logical_and(z >= 2, jnp.logical_not(ga_stays(panel))))
        def _():
            ga_copy(panel).wait_send()

    for gather in (fxx, fxy, gxx, gxy, f_gather, s_gather, p_gather, g_gather):
        gather.drain()
    fx_to_sibling.wait_send()
    gx_to_sibling.wait_send()
    for number, index in ((0, s_gather.down), (1, s_gather.up), (2, s_gather.far)):
        s_to_sibling(number, index).wait_send()
        g_to_sibling(number, index).wait_send()
    g_to_sibling(3, y).wait_send()


def on_device(*arrays):
    dma = pltpu.SemaphoreType.DMA
    any_space = pl.BlockSpec(memory_space=pl.ANY)
    scratch = [
        pltpu.VMEM((2, 512, 512), F32),
        pltpu.VMEM((2, 512, 512), F32),
        pltpu.VMEM((4, 384, 256), F32),
        pltpu.VMEM((8, 128, 256), F32),
        pltpu.VMEM((2, 2, 4, 4, 32, 128), F32),
        pltpu.VMEM((2, 4, 4, 32, 256), F32),
        pltpu.VMEM((2, 4, 4, 32, 384), F32),
        pltpu.VMEM((384, 1024), BF16),
        pltpu.VMEM((384, 1024), BF16),
        pltpu.VMEM((4, 2, 512, 256), F32),
        pltpu.VMEM((512, 256), BF16),
        pltpu.VMEM((512, 256), BF16),
        pltpu.VMEM((3, 2, 4, 4, 32, 256), F32),
        pltpu.VMEM((4, 384, 256), F32),
        pltpu.VMEM((4, 384, 256), F32),
        pltpu.VMEM((384, 1024), BF16),
        pltpu.VMEM((384, 1024), BF16),
        pltpu.VMEM((3, 384, 256), F32),
        dma((9,)),
        dma((8,)),
        dma((8,)),
        dma((4,)),
        dma((4,)),
        dma((7,)),
        dma((2,)),
        dma((7,)),
        dma((1,)),
        dma((4,)),
        dma((4,)),
        dma((4,)),
        dma((4,)),
        dma((4,)),
        dma((4,)),
        dma((4,)),
        dma((4,)),
        dma((2,)),
        dma((2,)),
        dma((3,)),
        dma((3,)),
        dma((4,)),
        dma((4,)),
        dma((3,)),
        dma((3,)),
        dma((2,)),
        dma((4, 2)),
        dma((8,)),
        dma((8,)),
        dma((4,)),
        dma((4,)),
        dma((4,)),
        dma((4,)),
        dma((4,)),
        dma((4,)),
        dma((3,)),
        dma((3,)),
        dma((4,)),
        dma((4,)),
        dma((4, 4)),
        dma((16,)),
    ]
    return pl.pallas_call(
        kernel,
        out_shape=jax.ShapeDtypeStruct((1536, 256), F32),
        in_specs=[any_space] * 5,
        out_specs=any_space,
        scratch_shapes=scratch,
        compiler_params=pltpu.CompilerParams(
            has_side_effects=True, vmem_limit_bytes=56 * 1024 * 1024
        ),
        name="two_sided_panels",
    )(*arrays)


def solution(mesh):
    return jax.shard_map(
        on_device,
        mesh=mesh,
        in_specs=(P("rows", "cols"), P(), P(None, "cols", "rows"), P(), P(None, "cols", "rows")),
        out_specs=P("cols", "rows"),
        check_vma=False,
    )
```

time: 587 us -> 169 us (0.29)
  the two profiles are of different devices: /device:TPU:1 before, /device:TPU:134 now
where the time goes in v1:
time: 169 us
  Pallas kernels  167 us (99%)
  local copies, waits for them, and re-layouts  2.65 us (2%)
    pallas_call x1, Pallas kernels, on_device(): pl.pallas_call(kernel, out_shape=jax.ShapeDtypeStruct((1536, 256), F32),...  167 us

profile of v1, /device:TPU:134, one launch (start us, length us, event | category | flops | bytes accessed | tf_op | source)
XLA Modules:
  0.0 169.2 jit_solution(14857685556437632861)
XLA Ops:
  0.0 166.5 %two_sided_panels.1 = f32[1536,256]{1,0:T(8,128)} custom-call(f32[1536,256]{1,0:T(8,128)} %slab.1, f32[2,512,512]{2,1,0:T(8,128)} %inverse1.1, f32[2,32,1536]{2,1,0:T(8,128)} %factor1.1, f32[2,512,512]{2,1,0:T(8,128)} %inverse2.1, f32[2,32,256]{2,1,0:T(8,128)} %factor2.1), custom_call_target="tpu_custom_call" | custom-call | tf_op jit(solution)/shard_map/two_sided_panels/pallas_call | solution.py:794
  166.5 2.7 %copy.7 = f32[1536,256]{1,0:T(8,128)} copy(f32[1536,256]{1,0:T(8,128)} %two_sided_panels.1) | data formatting | bytes 3145728

commit v2 on v1

v2 whole, which is shorter than its diff:
```python
import jax
import jax.numpy as jnp
from jax import lax
from jax.experimental import pallas as pl
from jax.experimental.pallas import tpu as pltpu
from jax.sharding import PartitionSpec as P

MESH = pl.DeviceIdType.MESH
F32 = jnp.float32
BF16 = jnp.bfloat16
NN = (((1,), (0,)), ((), ()))
NT = (((1,), (1,)), ((), ()))


def split(value):
    high = value.astype(BF16)
    return high, (value - high.astype(F32)).astype(BF16)


def product(a, b, dims=NN):
    def dot(u, v):
        return lax.dot_general(u, v, dims, preferred_element_type=F32)

    return dot(a[0], b[0]) + (dot(a[0], b[1]) + dot(a[1], b[0]))


def remote(src, dst, send_sem, recv_sem, device):
    return pltpu.make_async_remote_copy(
        src_ref=src,
        dst_ref=dst,
        send_sem=send_sem,
        recv_sem=recv_sem,
        device_id=device,
        device_id_type=MESH,
    )


class Gather4:
    def __init__(self, index, device, slot, half, send, recv, src=None):
        self.up, self.down, self.far = (index + 1) % 4, (index + 3) % 4, (index + 2) % 4
        self.slot = slot
        to_up, to_down = device(self.up), device(self.down)
        own = slot(index)
        self.first = [
            remote(own if src is None else src, own, send.at[0], recv.at[0], to_up),
            remote(own if src is None else src, own, send.at[1], recv.at[1], to_down),
        ]
        self.second = [
            remote(half(0, self.down), half(0, self.down), send.at[2], recv.at[2], to_up),
            remote(half(1, self.up), half(1, self.up), send.at[3], recv.at[3], to_down),
        ]
        self.landing = [
            remote(own, slot(self.down), send.at[0], recv.at[0], to_up),
            remote(own, slot(self.up), send.at[1], recv.at[1], to_down),
            remote(half(0, self.far), half(0, self.far), send.at[2], recv.at[2], to_up),
            remote(half(1, self.far), half(1, self.far), send.at[3], recv.at[3], to_down),
        ]

    def start(self):
        for copy in self.first:
            copy.start()

    def forward(self, then=None):
        for way in (0, 1):
            self.landing[way].wait_recv()
            self.second[way].start()
            if then is not None:
                then(way, (self.down, self.up)[way])

    def finish(self, then=None):
        self.landing[2].wait_recv()
        self.landing[3].wait_recv()
        if then is not None:
            then(2, self.far)

    def drain(self):
        for copy in self.first + self.second:
            copy.wait_send()


class Spread8:
    def __init__(self, z, device, is_source, block, up, down):
        self.z, self.is_source, self.block, self.up, self.down = z, is_source, block, up, down
        self.above, self.below = device((z + 1) % 8), device((z + 7) % 8)

    def source(self, event):
        return (self.z + 16 - event) % 8

    def copy(self, way, source, src=None):
        block = self.block(source)
        send, recv = self.up if way > 0 else self.down
        to = self.above if way > 0 else self.below
        return remote(
            block if src is None else src, block, send.at[source], recv.at[source], to
        )

    def landed(self, event, then=None, src=None):
        source = self.source(event)

        @pl.when(self.is_source(source))
        def _():
            if event != 0:
                self.copy(1 if event > 0 else -1, source).wait_recv()
            if 0 <= event < 4:
                self.copy(1, source, src).start()
            if -3 < event <= 0:
                self.copy(-1, source, src).start()
            if then is not None:
                then(source)

    def sent(self, event, then=None):
        source = self.source(event)

        @pl.when(self.is_source(source))
        def _():
            if 0 <= event < 4:
                self.copy(1, source).wait_send()
            if -3 < event <= 0:
                self.copy(-1, source).wait_send()
            if then is not None:
                then(source)


EVENTS = (0, 1, -1, 2, -2, 3, -3, 4)


def kernel(
    slab,
    inverse1,
    factor1,
    inverse2,
    factor2,
    out,
    i1,
    i2h,
    i2l,
    kh,
    kl,
    xt,
    xp,
    fx,
    gx,
    ft,
    wh,
    wl,
    vh,
    vl,
    gt,
    pb,
    zh,
    zl,
    db,
    eb,
    local,
    up_send,
    up_recv,
    down_send,
    down_recv,
    py_send,
    py_recv,
    xs_send,
    xs_recv,
    fz_send,
    fz_recv,
    gz_send,
    gz_recv,
    fxx_send,
    fxx_recv,
    fxy_send,
    fxy_recv,
    gxx_send,
    gxx_recv,
    gxy_send,
    gxy_recv,
    sib_send,
    sib_recv,
    fa_send,
    fa_recv,
    ft_send,
    ft_recv,
    xa_send,
    xa_recv,
    ga_send,
    ga_recv,
    gu_send,
    gu_recv,
    gd_send,
    gd_recv,
    gy_send,
    gy_recv,
    gs_send,
    gs_recv,
    p_send,
    p_recv,
    e_send,
    e_recv,
    o_send,
    o_recv,
):
    r = lax.axis_index("rows")
    c = lax.axis_index("cols")
    z, k = r // 2, r % 2
    y, x = c // 4, c % 4
    sibling = (2 * z + 1 - k, c)
    scope = jax.named_scope

    def along_y(index):
        return (r, 4 * index + x)

    def along_x(index):
        return (r, 4 * y + index)

    def along_z(index):
        return (2 * index + k, c)

    panel_rows = slab.at[pl.ds(0, 128), :]

    def in_panels(source):
        return source < 4

    def block_of(index, source, core=k):
        return xp.at[index, 2 * source + core]

    def xs_copy(number, index, source, src=None):
        block = block_of(index, source)
        return remote(
            block if src is None else src,
            block,
            xs_send.at[number, source],
            xs_recv.at[number, source],
            sibling,
        )

    def xs_landing(number, index, source):
        block = block_of(index, source, 1 - k)
        return remote(
            block, block, xs_send.at[number, source], xs_recv.at[number, source], sibling
        )

    def over_y(source, src=None):
        return Gather4(
            y,
            along_y,
            lambda index: block_of(index, source),
            lambda part, index: xp.at[index, 2 * source + k, pl.ds(64 * part, 64)],
            py_send.at[source],
            py_recv.at[source],
            src,
        )

    panels = Spread8(
        z,
        along_z,
        in_panels,
        lambda source: block_of(y, source),
        (up_send, up_recv),
        (down_send, down_recv),
    )

    def landed(event):
        src = panel_rows if event == 0 else None

        def then(source):
            over_y(source, src).start()
            xs_copy(0, y, source, src).start()

        panels.landed(event, then, src)

    def passed_on(event):
        source = panels.source(event)

        @pl.when(in_panels(source))
        def _():
            over_y(source).forward(
                then=lambda number, index: xs_copy(1 + number, index, source).start()
            )

    def arrived(event):
        source = panels.source(event)

        @pl.when(in_panels(source))
        def _():
            over_y(source).finish(
                then=lambda number, index: xs_copy(1 + number, index, source).start()
            )

    def sent(event):
        def then(source):
            over_y(source).drain()
            for number, index in ((0, y), (1, (y + 3) % 4), (2, (y + 1) % 4), (3, (y + 2) % 4)):
                xs_copy(number, index, source).wait_send()

        panels.sent(event, then)

    def own_panel():
        return pltpu.make_async_copy(panel_rows, block_of(y, z), local.at[0])

    with scope("barrier"):
        barrier = pltpu.get_barrier_semaphore()
        for distance in range(1, 4):
            over_x = (x + distance) % 4
            for device in (
                along_y((y + distance) % 4),
                along_x(over_x),
                (2 * z + 1 - k, 4 * y + over_x),
            ):
                pl.semaphore_signal(barrier, inc=1, device_id=device, device_id_type=MESH)
        for distance in range(1, 16):
            pl.semaphore_signal(
                barrier, inc=1, device_id=((r + distance) % 16, c), device_id_type=MESH
            )
        pl.semaphore_wait(barrier, 24)

    landed(0)

    @pl.when(in_panels(z))
    def _():
        own_panel().start()

    fz_src = factor1.at[0, :, pl.ds(0, 128)]
    gz_src = factor2.at[0]

    def fz_dst(which):
        return fx.at[k, which, y, x]

    gz_dst = gx.at[k, y, x]
    fz_own = pltpu.make_async_copy(fz_src, fz_dst(z % 2), local.at[1])
    gz_own = pltpu.make_async_copy(gz_src, gz_dst, local.at[2])
    f_source = jnp.logical_or(z == 2, z == 3)

    def fz_copy(distance):
        return remote(
            fz_src,
            fz_dst(z % 2),
            fz_send.at[distance - 1],
            fz_recv.at[z % 2],
            along_z((z + distance) % 8),
        )

    def gz_copy(distance):
        return remote(
            gz_src, gz_dst, gz_send.at[distance - 1], gz_recv.at[0], along_z((z + distance) % 8)
        )

    @pl.when(f_source)
    def _():
        fz_own.start()
        for distance in range(1, 8):
            fz_copy(distance).start()

    def fa_copy(distance):
        to = (y + distance) % 4
        columns = pl.ds(pl.multiple_of(to * 384, 128), 384)
        return remote(
            factor1.at[:, :, columns],
            ft.at[:, y, x],
            fa_send.at[distance - 1],
            fa_recv.at[distance - 1],
            along_y(to),
        )

    fa_own = pltpu.make_async_copy(
        factor1.at[:, :, pl.ds(pl.multiple_of(y * 384, 128), 384)], ft.at[:, y, x], local.at[3]
    )
    fa_own.start()
    for distance in (2, 1, 3):
        fa_copy(distance).start()

    load1 = pltpu.make_async_copy(inverse1, i1, local.at[5])
    load1.start()

    @pl.when(z == 1)
    def _():
        gz_own.start()
        for distance in range(1, 8):
            gz_copy(distance).start()

    g_plane = r % 4
    g_block = r // 4

    def ga_copy(panel):
        return remote(
            factor2.at[panel],
            gt.at[g_block - 1, panel, y, x],
            ga_send.at[panel],
            ga_recv.at[x, k],
            (2 * z + panel, 4 * y + g_plane),
        )

    def ga_own(panel):
        return pltpu.make_async_copy(
            factor2.at[panel], gt.at[g_block - 1, panel, y, x], local.at[7]
        )

    def ga_stays(panel):
        return jnp.logical_and(g_plane == x, k == panel)

    for panel in (0, 1):

        @pl.when(jnp.logical_and(z >= 2, ga_stays(panel)))
        def _():
            ga_own(panel).start()

        @pl.when(jnp.logical_and(z >= 2, jnp.logical_not(ga_stays(panel))))
        def _():
            ga_copy(panel).start()

    def g_source(source):
        return jnp.logical_and(source >= 2, source % 2 == x // 2)

    g_spread = Spread8(
        z,
        along_z,
        g_source,
        lambda source: gt.at[source // 2 - 1, k, y],
        (gu_send, gu_recv),
        (gd_send, gd_recv),
    )

    def g_slot(index):
        return gt.at[:, k, index]

    def g_to_sibling(number, index):
        return remote(g_slot(index), g_slot(index), gs_send.at[number], gs_recv.at[number], sibling)

    def g_from_sibling(number, index):
        theirs = gt.at[:, 1 - k, index]
        return remote(theirs, theirs, gs_send.at[number], gs_recv.at[number], sibling)

    g_gather = Gather4(
        y,
        along_y,
        g_slot,
        lambda part, index: gt.at[:, k, index, pl.ds(2 * part, 2)],
        gy_send,
        gy_recv,
    )

    def xa_copy(distance):
        to = (y + distance) % 4
        return remote(
            slab.at[pl.ds(pl.multiple_of(to * 384, 128), 384), :],
            xt.at[y],
            xa_send.at[distance - 1],
            xa_recv.at[distance - 1],
            along_y(to),
        )

    xa_own = pltpu.make_async_copy(
        slab.at[pl.ds(pl.multiple_of(y * 384, 128), 384), :], xt.at[y], local.at[4]
    )

    fxy = Gather4(
        y,
        along_y,
        lambda index: fx.at[k, :, index, x],
        lambda part, index: fx.at[k, part, index, x],
        fxy_send,
        fxy_recv,
    )
    fxx = Gather4(
        x,
        along_x,
        lambda index: fx.at[k, :, :, index],
        lambda part, index: fx.at[k, part, :, index],
        fxx_send,
        fxx_recv,
    )
    gxy = Gather4(
        y,
        along_y,
        lambda index: gx.at[k, index, x],
        lambda part, index: gx.at[k, index, x, pl.ds(16 * part, 16)],
        gxy_send,
        gxy_recv,
    )
    gxx = Gather4(
        x,
        along_x,
        lambda index: gx.at[k, :, index],
        lambda part, index: gx.at[k, pl.ds(2 * part, 2), index],
        gxx_send,
        gxx_recv,
    )
    f_gather = Gather4(
        x,
        along_x,
        lambda index: ft.at[:, :, index],
        lambda part, index: ft.at[part, :, index],
        ft_send,
        ft_recv,
    )
    fx_to_sibling = remote(fx.at[k], fx.at[k], sib_send.at[0], sib_recv.at[0], sibling)
    gx_to_sibling = remote(gx.at[k], gx.at[k], sib_send.at[1], sib_recv.at[1], sibling)
    fx_from_sibling = remote(fx.at[1 - k], fx.at[1 - k], sib_send.at[0], sib_recv.at[0], sibling)
    gx_from_sibling = remote(gx.at[1 - k], gx.at[1 - k], sib_send.at[1], sib_recv.at[1], sibling)

    with scope("wait_panels_1"):
        landed(1)
        landed(-1)
    with scope("pass_panels_0"):
        passed_on(0)
    with scope("wait_coupling_z"):
        for which in (0, 1):

            @pl.when(z == 2 + which)
            def _():
                fz_own.wait()

            @pl.when(z != 2 + which)
            def _():
                remote(
                    fz_src, fz_dst(which), fz_send.at[0], fz_recv.at[which], sibling
                ).wait_recv()

        fxy.start()

        @pl.when(z == 1)
        def _():
            gz_own.wait()

        @pl.when(z != 1)
        def _():
            remote(gz_src, gz_dst, gz_send.at[0], gz_recv.at[0], sibling).wait_recv()

        gxy.start()
    with scope("wait_panels_2"):
        landed(2)
        landed(-2)
    with scope("pass_panels_1"):
        passed_on(1)
        passed_on(-1)
    with scope("wait_first_factor_y"):
        fa_own.wait()
        for distance in (1, 3, 2):
            remote(
                ft.at[:, y, x],
                ft.at[:, (y + 4 - distance) % 4, x],
                fa_send.at[distance - 1],
                fa_recv.at[distance - 1],
                sibling,
            ).wait_recv()
    f_gather.start()
    with scope("pass_coupling_y"):
        fxy.forward()
        gxy.forward()
    with scope("wait_panels_3"):
        landed(3)
        landed(-3)
    with scope("pass_panels_2"):
        passed_on(2)
        passed_on(-2)
    xa_own.start()

    @pl.when(y == 0)
    def _():
        for distance in (2, 1, 3):
            xa_copy(distance).start()

    with scope("finish_coupling_y"):
        fxy.finish()
        fxx.start()
        gxy.finish()
        gxx.start()
    with scope("wait_panels_4"):
        landed(4)
    with scope("pass_panels_3"):
        passed_on(3)
        passed_on(-3)
    with scope("wait_second_factor_x"):

        @pl.when(g_source(z))
        def _():
            for source_x in range(4):
                stays = jnp.logical_and(source_x == x, k == x % 2)
                block = gt.at[z // 2 - 1, k, y, source_x]

                @pl.when(stays)
                def _():
                    pltpu.make_async_copy(factor2.at[k], block, local.at[7]).wait()

                @pl.when(jnp.logical_not(stays))
                def _():
                    remote(
                        block, block, ga_send.at[0], ga_recv.at[source_x, x % 2], sibling
                    ).wait_recv()

    g_spread.landed(0)
    with scope("pass_coupling_x"):
        fxx.forward()
        gxx.forward()
    with scope("pass_panels_4"):
        passed_on(4)

    @pl.when(y != 0)
    def _():
        for distance in (2, 1, 3):
            xa_copy(distance).start()

    with scope("pass_first_factor"):
        f_gather.forward()
    with scope("finish_coupling_x"):
        fxx.finish()
        fx_to_sibling.start()
        gxx.finish()
        gx_to_sibling.start()
    with scope("finish_first_factor"):
        f_gather.finish()

    has_panel_rows = jnp.logical_and(y == 0, r < 8)
    with scope("turn_first_factor"):
        for panel in (0, 1):
            for part in range(4):
                high, rest = split(ft[panel, part].reshape(128, 384).T)
                at = (4 * panel + part) * 128
                wh[:, at : at + 128] = high
                wl[:, at : at + 128] = rest

        @pl.when(has_panel_rows)
        def _():
            row = lax.broadcasted_iota(jnp.int32, (128, 1024), 0)
            column = lax.broadcasted_iota(jnp.int32, (128, 1024), 1)
            unit = jnp.where(column == row + r * 128, -1.0, 0.0)
            wh[pl.ds(0, 128), :] = unit.astype(BF16)
            wl[pl.ds(0, 128), :] = jnp.zeros((128, 1024), BF16)

    with scope("wait_second_factor_1"):
        g_spread.landed(1)
        g_spread.landed(-1)
    with scope("wait_coupling_core"):
        load1.wait()
        fx_from_sibling.wait_recv()

    with scope("left_operator"):
        value1 = split(product((wh[:, 512:], wl[:, 512:]), split(i1[1])))
        vh[:, 512:], vl[:, 512:] = value1
        value0 = wh[:, :512].astype(F32) + wl[:, :512].astype(F32)
        for number in range(4):
            at = 512 + 128 * number
            value0 = value0 - product(
                (vh[:, at : at + 128], vl[:, at : at + 128]),
                split(fx[number % 2, number // 2].reshape(512, 128)),
                NT,
            )
        vh[:, :512], vl[:, :512] = split(product(split(value0), split(i1[0])))

    load2 = pltpu.make_async_copy(inverse2, i1, local.at[6])
    load2.start()
    with scope("wait_second_factor_2"):
        g_spread.landed(2)
        g_spread.landed(-2)
    with scope("finish_panels"):
        for event in EVENTS:
            arrived(event)

    def wait_slab(distance):
        remote(
            xt.at[y],
            xt.at[(y + 4 - distance) % 4],
            xa_send.at[distance - 1],
            xa_recv.at[distance - 1],
            sibling,
        ).wait_recv()

    def left(block):
        rows = split(xp[block].reshape(1024, 256))
        return xt[block] - product((vh[...], vl[...]), rows)

    def wait_panel_core(number, index):
        for source in range(4):
            xs_landing(number, index, source).wait_recv()

    with scope("wait_slab_0"):
        for distance in (1, 2, 3):

            @pl.when(y == distance)
            def _():
                wait_slab(distance)

        @pl.when(y == 0)
        def _():
            xa_own.wait()

    with scope("wait_panels_core"):
        @pl.when(in_panels(z))
        def _():
            own_panel().wait()

        for number, index in ((0, y), (1, (y + 3) % 4), (2, (y + 1) % 4), (3, (y + 2) % 4)):
            wait_panel_core(number, index)

    @pl.when(has_panel_rows)
    def _():
        xt[0, pl.ds(0, 128)] = jnp.zeros((128, 256), F32)

    with scope("left_update_0"):
        pb[x] = left(0)

    p_gather = Gather4(
        x,
        along_x,
        lambda index: pb.at[index],
        lambda part, index: pb.at[index, pl.ds(192 * part, 192)],
        p_send,
        p_recv,
    )
    p_gather.start()
    with scope("wait_right_operator"):
        load2.wait()
        gx_from_sibling.wait_recv()
    with scope("right_operator"):
        for panel in (0, 1):
            i2h[panel], i2l[panel] = split(i1[panel])
        total = None
        for part in (0, 1):
            at = 256 * part
            term = product(
                (i2h[1, :, at : at + 256], i2l[1, :, at : at + 256]),
                split(gx[part].reshape(512, 256)),
                NT,
            )
            total = term if total is None else total + term
        kh[...], kl[...] = split(product(split(total), (i2h[0], i2l[0])))

    with scope("wait_second_factor_3"):
        g_spread.landed(3)
        g_spread.landed(-3)
        g_spread.landed(4)
    g_gather.start()
    g_to_sibling(3, y).start()
    with scope("pass_columns"):
        p_gather.forward()
    with scope("wait_slab_rest"):
        for distance in (1, 2, 3):

            @pl.when(y != distance)
            def _():
                wait_slab(distance)

        @pl.when(y != 0)
        def _():
            xa_own.wait()

        @pl.when(has_panel_rows)
        def _():
            for block in range(1, 4):
                xt[block, pl.ds(0, 128)] = jnp.zeros((128, 256), F32)

    with scope("left_update_rest"):

        @pl.loop(1, 4)
        def _(block):
            db[block] = left(block)

    with scope("pass_second_factor"):
        g_gather.forward(then=lambda number, index: g_to_sibling(number, index).start())

    with scope("finish_columns"):
        p_gather.finish()

    with scope("solve_columns"):
        for half in (0, 1):
            rows = pl.ds(256 * half, 256)
            first = None
            second = None
            for part in range(2):
                at = 256 * part
                left0 = split(pb[part])
                left1 = split(pb[2 + part])
                term0 = product(left0, (i2h[0, rows, at : at + 256], i2l[0, rows, at : at + 256]), NT)
                term1 = product(
                    left1, (i2h[1, rows, at : at + 256], i2l[1, rows, at : at + 256]), NT
                ) - product(left0, (kh[rows, at : at + 256], kl[rows, at : at + 256]), NT)
                first = term0 if first is None else first + term0
                second = term1 if second is None else second + term1
            for number, value in ((half, first), (2 + half, second)):
                at = 256 * number
                zh[:, at : at + 256], zl[:, at : at + 256] = split(value)

                @pl.when(x == number)
                def _():
                    db[0] = value

    out_rows = out.at[pl.ds(pl.multiple_of(r * 96, 32), 96), :]

    def own_rows_of(block):
        return db.at[block, pl.ds(pl.multiple_of(96 * x, 32), 96)]

    def turn_x(block, distance):
        to = (x + distance) % 4
        return remote(
            db.at[block, pl.ds(pl.multiple_of(96 * to, 32), 96)],
            eb.at[x, block],
            e_send.at[block, distance - 1],
            e_recv.at[block, distance - 1],
            along_x(to),
        )

    def turn_z(block, distance, remote_do, local_do):
        from_x = (x + 4 - distance) % 4
        src = own_rows_of(block) if distance == 0 else eb.at[from_x, block]
        to = 4 * block + from_x

        @pl.when(to == r)
        def _():
            local_do(pltpu.make_async_copy(src, out_rows, local.at[8]))

        @pl.when(to != r)
        def _():
            remote_do(
                remote(src, out_rows, o_send.at[block, distance], o_recv.at[r], (to, c))
            )

    def start(copy):
        copy.start()

    with scope("finish_second_factor"):
        g_gather.finish(then=lambda number, index: g_to_sibling(number, index).start())
        for number, index in ((3, y), (0, g_gather.down), (1, g_gather.up), (2, g_gather.far)):
            g_from_sibling(number, index).wait_recv()
    with scope("right_update"):
        for turn in (2, 1, 3, 0):
            block = (z // 2 + turn) % 4

            @pl.when(block != 0)
            def _():
                factor = split(gt[block - 1].reshape(1024, 256))
                db[block] = db[block] - product((zh[...], zl[...]), factor)

            for distance in (2, 1, 3):
                turn_x(block, distance).start()
            turn_z(block, 0, start, start)
    with scope("pass_out"):
        for turn in (2, 1, 3, 0):
            block = (z // 2 + turn) % 4
            for distance in (1, 3, 2):
                here = eb.at[(x + 4 - distance) % 4, block]
                remote(
                    here,
                    here,
                    e_send.at[block, distance - 1],
                    e_recv.at[block, distance - 1],
                    sibling,
                ).wait_recv()
                turn_z(block, distance, start, start)

    with scope("wait_out"):
        for source in range(16):
            rows = out.at[pl.ds(96 * source, 96), :]

            @pl.when(source != r)
            def _():
                remote(rows, rows, o_send.at[0, 0], o_recv.at[source], sibling).wait_recv()

    with scope("drain"):
        for block in range(4):
            for distance in range(4):
                turn_z(block, distance, lambda copy: copy.wait_send(), lambda copy: copy.wait())
            for distance in (1, 2, 3):
                turn_x(block, distance).wait_send()
        for event in EVENTS:
            sent(event)
            g_spread.sent(event)

        @pl.when(f_source)
        def _():
            for distance in range(1, 8):
                fz_copy(distance).wait_send()

        @pl.when(z == 1)
        def _():
            for distance in range(1, 8):
                gz_copy(distance).wait_send()

        for distance in (1, 2, 3):
            fa_copy(distance).wait_send()
            xa_copy(distance).wait_send()
        for panel in (0, 1):

            @pl.when(jnp.logical_and(z >= 2, jnp.logical_not(ga_stays(panel))))
            def _():
                ga_copy(panel).wait_send()

        for gather in (fxx, fxy, gxx, gxy, f_gather, p_gather, g_gather):
            gather.drain()
        fx_to_sibling.wait_send()
        gx_to_sibling.wait_send()
        for number, index in ((3, y), (0, g_gather.down), (1, g_gather.up), (2, g_gather.far)):
            g_to_sibling(number, index).wait_send()


def on_device(*arrays):
    dma = pltpu.SemaphoreType.DMA
    any_space = pl.BlockSpec(memory_space=pl.ANY)
    scratch = [
        pltpu.VMEM((2, 512, 512), F32),
        pltpu.VMEM((2, 512, 512), BF16),
        pltpu.VMEM((2, 512, 512), BF16),
        pltpu.VMEM((512, 512), BF16),
        pltpu.VMEM((512, 512), BF16),
        pltpu.VMEM((4, 384, 256), F32),
        pltpu.VMEM((4, 8, 128, 256), F32),
        pltpu.VMEM((2, 2, 4, 4, 32, 128), F32),
        pltpu.VMEM((2, 4, 4, 32, 256), F32),
        pltpu.VMEM((2, 4, 4, 32, 384), F32),
        pltpu.VMEM((384, 1024), BF16),
        pltpu.VMEM((384, 1024), BF16),
        pltpu.VMEM((384, 1024), BF16),
        pltpu.VMEM((384, 1024), BF16),
        pltpu.VMEM((3, 2, 4, 4, 32, 256), F32),
        pltpu.VMEM((4, 384, 256), F32),
        pltpu.VMEM((384, 1024), BF16),
        pltpu.VMEM((384, 1024), BF16),
        pltpu.VMEM((4, 384, 256), F32),
        pltpu.VMEM((4, 4, 96, 256), F32),
        dma((9,)),
        dma((4,)),
        dma((4,)),
        dma((4,)),
        dma((4,)),
        dma((4, 4)),
        dma((4, 4)),
        dma((4, 4)),
        dma((4, 4)),
        dma((7,)),
        dma((2,)),
        dma((7,)),
        dma((1,)),
        dma((4,)),
        dma((4,)),
        dma((4,)),
        dma((4,)),
        dma((4,)),
        dma((4,)),
        dma((4,)),
        dma((4,)),
        dma((2,)),
        dma((2,)),
        dma((3,)),
        dma((3,)),
        dma((4,)),
        dma((4,)),
        dma((3,)),
        dma((3,)),
        dma((2,)),
        dma((4, 2)),
        dma((8,)),
        dma((8,)),
        dma((8,)),
        dma((8,)),
        dma((4,)),
        dma((4,)),
        dma((4,)),
        dma((4,)),
        dma((4,)),
        dma((4,)),
        dma((4, 3)),
        dma((4, 3)),
        dma((4, 4)),
        dma((16,)),
    ]
    return pl.pallas_call(
        kernel,
        out_shape=jax.ShapeDtypeStruct((1536, 256), F32),
        in_specs=[any_space] * 5,
        out_specs=any_space,
        scratch_shapes=scratch,
        compiler_params=pltpu.CompilerParams(
            has_side_effects=True, collective_id=0, vmem_limit_bytes=56 * 1024 * 1024
        ),
        name="two_sided_panels",
    )(*arrays)


def solution(mesh):
    return jax.shard_map(
        on_device,
        mesh=mesh,
        in_specs=(P("rows", "cols"), P(), P(None, "cols", "rows"), P(), P(None, "cols", "rows")),
        out_specs=P("cols", "rows"),
        check_vma=False,
    )
```

time: 169 us -> 130 us (0.77)
  the two profiles are of different devices: /device:TPU:134 before, /device:TPU:1 now
where the time goes in v2:
time: 130 us; the launch traced here: 128 us
  Pallas kernels  125 us (96%)
  local copies, waits for them, and re-layouts  2.65 us (2%)
    pallas_call x1, Pallas kernels, on_device(): pl.pallas_call(kernel, out_shape=jax.ShapeDtypeStruct((1536, 256), F32),...  125 us
    unnamed x1, local copies, waits for them, and re-layouts  2.65 us

profile of v2, /device:TPU:1, one launch (start us, length us, event | category | flops | bytes accessed | tf_op | source)
XLA Modules:
  0.0 127.9 jit_solution(5133899007122039077)
XLA Ops:
  0.0 125.3 %two_sided_panels.1 = f32[1536,256]{1,0:T(8,128)} custom-call(f32[1536,256]{1,0:T(8,128)} %slab.1, f32[2,512,512]{2,1,0:T(8,128)} %inverse1.1, f32[2,32,1536]{2,1,0:T(8,128)} %factor1.1, f32[2,512,512]{2,1,0:T(8,128)} %inverse2.1, f32[2,32,256]{2,1,0:T(8,128)} %factor2.1), custom_call_target="tpu_custom_call" | custom-call | tf_op jit(solution)/shard_map/two_sided_panels/pallas_call | solution.py:962
  125.3 2.7 %copy.7 = f32[1536,256]{1,0:T(8,128)} copy(f32[1536,256]{1,0:T(8,128)} %two_sided_panels.1) | data formatting | bytes 3145728

commit v3 on v2

--- a/solution.py
+++ b/solution.py
@@ -122,6 +122,98 @@
 
 
 EVENTS = (0, 1, -1, 2, -2, 3, -3, 4)
+
+
+class Flow:
+    def __init__(self, z, y, k, is_source, key, block, half, devices, sems):
+        self.z, self.y, self.k, self.is_source, self.key = z, y, k, is_source, key
+        self.block, self.half = block, half
+        self.along_y, self.sibling = devices[1], devices[2]
+        self.up, self.down, self.over, self.core = sems
+        self.spread = Spread8(
+            z,
+            devices[0],
+            is_source,
+            lambda source: block(y, source, k),
+            self.up,
+            self.down,
+        )
+
+    def indices(self):
+        return self.y, (self.y + 3) % 4, (self.y + 1) % 4, (self.y + 2) % 4
+
+    def gather(self, source, src=None):
+        key = self.key(source)
+        return Gather4(
+            self.y,
+            self.along_y,
+            lambda index: self.block(index, source, self.k),
+            lambda part, index: self.half(part, index, source),
+            self.over[0].at[key],
+            self.over[1].at[key],
+            src,
+        )
+
+    def to_core(self, number, source, core, src=None):
+        block = self.block(self.indices()[number], source, core)
+        send, recv = self.core
+        key = self.key(source)
+        return remote(
+            block if src is None else src,
+            block,
+            send.at[number, key],
+            recv.at[number, key],
+            self.sibling,
+        )
+
+    def landed(self, *events, src=None, over=True):
+        def then(source):
+            if over:
+                self.gather(source, src).start()
+            self.to_core(0, source, self.k, src).start()
+
+        for event in events:
+            self.spread.landed(event, then, src)
+
+    def go_over(self, *events):
+        for event in events:
+            source = self.spread.source(event)
+
+            @pl.when(self.is_source(source))
+            def _():
+                self.gather(source).start()
+
+    def passed(self, *events):
+        for event in events:
+            source = self.spread.source(event)
+
+            @pl.when(self.is_source(source))
+            def _():
+                self.gather(source).forward(
+                    then=lambda number, index: self.to_core(1 + number, source, self.k).start()
+                )
+
+    def arrived(self, *events):
+        for event in events:
+            source = self.spread.source(event)
+
+            @pl.when(self.is_source(source))
+            def _():
+                self.gather(source).finish(
+                    then=lambda number, index: self.to_core(1 + number, source, self.k).start()
+                )
+
+    def wait_core(self, number, source):
+        self.to_core(number, source, 1 - self.k).wait_recv()
+
+    def sent(self):
+        def then(source):
+            self.gather(source).drain()
+            for number in range(4):
+                self.to_core(number, source, self.k).wait_send()
+
+        for event in EVENTS:
+            self.spread.sent(event, then)
 
 
 def kernel(
@@ -218,82 +310,20 @@
     def in_panels(source):
         return source < 4
 
-    def block_of(index, source, core=k):
-        return xp.at[index, 2 * source + core]
-
-    def xs_copy(number, index, source, src=None):
-        block = block_of(index, source)
-        return remote(
-            block if src is None else src,
-            block,
-            xs_send.at[number, source],
-            xs_recv.at[number, source],
-            sibling,
-        )
-
-    def xs_landing(number, index, source):
-        block = block_of(index, source, 1 - k)
-        return remote(
-            block, block, xs_send.at[number, source], xs_recv.at[number, source], sibling
-        )
-
-    def over_y(source, src=None):
-        return Gather4(
-            y,
-            along_y,
-            lambda index: block_of(index, source),
-            lambda part, index: xp.at[index, 2 * source + k, pl.ds(64 * part, 64)],
-            py_send.at[source],
-            py_recv.at[source],
-            src,
-        )
-
-    panels = Spread8(
+    panels = Flow(
         z,
-        along_z,
+        y,
+        k,
         in_panels,
-        lambda source: block_of(y, source),
-        (up_send, up_recv),
-        (down_send, down_recv),
-    )
-
-    def landed(event):
-        src = panel_rows if event == 0 else None
-
-        def then(source):
-            over_y(source, src).start()
-            xs_copy(0, y, source, src).start()
-
-        panels.landed(event, then, src)
-
-    def passed_on(event):
-        source = panels.source(event)
-
-        @pl.when(in_panels(source))
-        def _():
-            over_y(source).forward(
-                then=lambda number, index: xs_copy(1 + number, index, source).start()
-            )
-
-    def arrived(event):
-        source = panels.source(event)
-
-        @pl.when(in_panels(source))
-        def _():
-            over_y(source).finish(
-                then=lambda number, index: xs_copy(1 + number, index, source).start()
-            )
-
-    def sent(event):
-        def then(source):
-            over_y(source).drain()
-            for number, index in ((0, y), (1, (y + 3) % 4), (2, (y + 1) % 4), (3, (y + 2) % 4)):
-                xs_copy(number, index, source).wait_send()
-
-        panels.sent(event, then)
+        lambda source: source,
+        lambda index, source, core: xp.at[index, 2 * source + core],
+        lambda part, index, source: xp.at[index, 2 * source + k, pl.ds(64 * part, 64)],
+        (along_z, along_y, sibling),
+        ((up_send, up_recv), (down_send, down_recv), (py_send, py_recv), (xs_send, xs_recv)),
+    )
 
     def own_panel():
-        return pltpu.make_async_copy(panel_rows, block_of(y, z), local.at[0])
+        return pltpu.make_async_copy(panel_rows, xp.at[y, 2 * z + k], local.at[0])
 
     with scope("barrier"):
         barrier = pltpu.get_barrier_semaphore()
@@ -311,7 +341,7 @@
             )
         pl.semaphore_wait(barrier, 24)
 
-    landed(0)
+    panels.landed(0, src=panel_rows)
 
     @pl.when(in_panels(z))
     def _():
@@ -408,32 +438,16 @@
     def g_source(source):
         return jnp.logical_and(source >= 2, source % 2 == x // 2)
 
-    g_spread = Spread8(
+    seconds = Flow(
         z,
-        along_z,
+        y,
+        k,
         g_source,
-        lambda source: gt.at[source // 2 - 1, k, y],
-        (gu_send, gu_recv),
-        (gd_send, gd_recv),
-    )
-
-    def g_slot(index):
-        return gt.at[:, k, index]
-
-    def g_to_sibling(number, index):
-        return remote(g_slot(index), g_slot(index), gs_send.at[number], gs_recv.at[number], sibling)
-
-    def g_from_sibling(number, index):
-        theirs = gt.at[:, 1 - k, index]
-        return remote(theirs, theirs, gs_send.at[number], gs_recv.at[number], sibling)
-
-    g_gather = Gather4(
-        y,
-        along_y,
-        g_slot,
-        lambda part, index: gt.at[:, k, index, pl.ds(2 * part, 2)],
-        gy_send,
-        gy_recv,
+        lambda source: source // 2 - 1,
+        lambda index, source, core: gt.at[source // 2 - 1, core, index],
+        lambda part, index, source: gt.at[source // 2 - 1, k, index, pl.ds(2 * part, 2)],
+        (along_z, along_y, sibling),
+        ((gu_send, gu_recv), (gd_send, gd_recv), (gy_send, gy_recv), (gs_send, gs_recv)),
     )
 
     def xa_copy(distance):
@@ -495,42 +509,10 @@
     fx_from_sibling = remote(fx.at[1 - k], fx.at[1 - k], sib_send.at[0], sib_recv.at[0], sibling)
     gx_from_sibling = remote(gx.at[1 - k], gx.at[1 - k], sib_send.at[1], sib_recv.at[1], sibling)
 
-    with scope("wait_panels_1"):
-        landed(1)
-        landed(-1)
-    with scope("pass_panels_0"):
-        passed_on(0)
-    with scope("wait_coupling_z"):
-        for which in (0, 1):
-
-            @pl.when(z == 2 + which)
-            def _():
-                fz_own.wait()
-
-            @pl.when(z != 2 + which)
-            def _():
-                remote(
-                    fz_src, fz_dst(which), fz_send.at[0], fz_recv.at[which], sibling
-                ).wait_recv()
-
-        fxy.start()
-
-        @pl.when(z == 1)
-        def _():
-            gz_own.wait()
-
-        @pl.when(z != 1)
-        def _():
-            remote(gz_src, gz_dst, gz_send.at[0], gz_recv.at[0], sibling).wait_recv()
-
-        gxy.start()
-    with scope("wait_panels_2"):
-        landed(2)
-        landed(-2)
-    with scope("pass_panels_1"):
-        passed_on(1)
-        passed_on(-1)
-    with scope("wait_first_factor_y"):
+    with scope("panels_1"):
+        panels.landed(1, -1)
+        panels.passed(0)
+    with scope("first_factor_y"):
         fa_own.wait()
         for distance in (1, 3, 2):
             remote(
@@ -541,33 +523,54 @@
                 sibling,
             ).wait_recv()
     f_gather.start()
+    with scope("coupling_z"):
+        for which in (0, 1):
+
+            @pl.when(z == 2 + which)
+            def _():
+                fz_own.wait()
+
+            @pl.when(z != 2 + which)
+            def _():
+                remote(
+                    fz_src, fz_dst(which), fz_send.at[0], fz_recv.at[which], sibling
+                ).wait_recv()
+
+    fxy.start()
+    with scope("second_coupling_z"):
+
+        @pl.when(z == 1)
+        def _():
+            gz_own.wait()
+
+        @pl.when(z != 1)
+        def _():
+            remote(gz_src, gz_dst, gz_send.at[0], gz_recv.at[0], sibling).wait_recv()
+
+    gxy.start()
+    with scope("panels_2"):
+        panels.landed(2, -2)
+        panels.passed(1, -1)
     with scope("pass_coupling_y"):
         fxy.forward()
         gxy.forward()
-    with scope("wait_panels_3"):
-        landed(3)
-        landed(-3)
-    with scope("pass_panels_2"):
-        passed_on(2)
-        passed_on(-2)
-    xa_own.start()
-
-    @pl.when(y == 0)
-    def _():
-        for distance in (2, 1, 3):
-            xa_copy(distance).start()
-
+    with scope("panels_3"):
+        panels.landed(3, -3)
+        panels.passed(2, -2)
     with scope("finish_coupling_y"):
         fxy.finish()
-        fxx.start()
+    fxx.start()
+    with scope("pass_first_factor"):
+        f_gather.forward()
+    with scope("panels_4"):
+        panels.landed(4)
+        panels.passed(3, -3)
+    with scope("finish_second_coupling_y"):
         gxy.finish()
-        gxx.start()
-    with scope("wait_panels_4"):
-        landed(4)
-    with scope("pass_panels_3"):
-        passed_on(3)
-        passed_on(-3)
-    with scope("wait_second_factor_x"):
+    gxx.start()
+    with scope("pass_coupling_x"):
+        fxx.forward()
+    with scope("second_factor_x"):
 
         @pl.when(g_source(z))
         def _():
@@ -585,25 +588,21 @@
                         block, block, ga_send.at[0], ga_recv.at[source_x, x % 2], sibling
                     ).wait_recv()
 
-    g_spread.landed(0)
-    with scope("pass_coupling_x"):
-        fxx.forward()
-        gxx.forward()
+    seconds.landed(0, over=False)
     with scope("pass_panels_4"):
-        passed_on(4)
+        panels.passed(4)
+    xa_own.start()
+
+    @pl.when(y == 0)
+    def _():
+        for distance in (2, 1, 3):
+            xa_copy(distance).start()
 
     @pl.when(y != 0)
     def _():
         for distance in (2, 1, 3):
             xa_copy(distance).start()
 
-    with scope("pass_first_factor"):
-        f_gather.forward()
-    with scope("finish_coupling_x"):
-        fxx.finish()
-        fx_to_sibling.start()
-        gxx.finish()
-        gx_to_sibling.start()
     with scope("finish_first_factor"):
         f_gather.finish()
 
@@ -624,10 +623,16 @@
             wh[pl.ds(0, 128), :] = unit.astype(BF16)
             wl[pl.ds(0, 128), :] = jnp.zeros((128, 1024), BF16)
 
-    with scope("wait_second_factor_1"):
-        g_spread.landed(1)
-        g_spread.landed(-1)
-    with scope("wait_coupling_core"):
+    with scope("finish_coupling_x"):
+        fxx.finish()
+    fx_to_sibling.start()
+    with scope("pass_second_coupling_x"):
+        gxx.forward()
+    with scope("seconds_1"):
+        seconds.landed(1, -1, over=False)
+    with scope("arrived_panels_1"):
+        panels.arrived(0, 1, -1)
+    with scope("coupling_core"):
         load1.wait()
         fx_from_sibling.wait_recv()
 
@@ -646,12 +651,14 @@
 
     load2 = pltpu.make_async_copy(inverse2, i1, local.at[6])
     load2.start()
-    with scope("wait_second_factor_2"):
-        g_spread.landed(2)
-        g_spread.landed(-2)
-    with scope("finish_panels"):
-        for event in EVENTS:
-            arrived(event)
+    with scope("finish_second_coupling_x"):
+        gxx.finish()
+    gx_to_sibling.start()
+    with scope("arrived_panels_2"):
+        panels.arrived(2, -2, 3, -3, 4)
+    with scope("seconds_2"):
+        seconds.landed(2, -2, over=False)
+    seconds.go_over(0, 1, -1, 2, -2)
 
     def wait_slab(distance):
         remote(
@@ -666,10 +673,6 @@
         rows = split(xp[block].reshape(1024, 256))
         return xt[block] - product((vh[...], vl[...]), rows)
 
-    def wait_panel_core(number, index):
-        for source in range(4):
-            xs_landing(number, index, source).wait_recv()
-
     with scope("wait_slab_0"):
         for distance in (1, 2, 3):
 
@@ -686,8 +689,9 @@
         def _():
             own_panel().wait()
 
-        for number, index in ((0, y), (1, (y + 3) % 4), (2, (y + 1) % 4), (3, (y + 2) % 4)):
-            wait_panel_core(number, index)
+        for number in range(4):
+            for source in range(4):
+                panels.wait_core(number, source)
 
     @pl.when(has_panel_rows)
     def _():
@@ -705,6 +709,8 @@
         p_recv,
     )
     p_gather.start()
+    with scope("seconds_3"):
+        seconds.landed(3, -3)
     with scope("wait_right_operator"):
         load2.wait()
         gx_from_sibling.wait_recv()
@@ -722,12 +728,8 @@
             total = term if total is None else total + term
         kh[...], kl[...] = split(product(split(total), (i2h[0], i2l[0])))
 
-    with scope("wait_second_factor_3"):
-        g_spread.landed(3)
-        g_spread.landed(-3)
-        g_spread.landed(4)
-    g_gather.start()
-    g_to_sibling(3, y).start()
+    with scope("seconds_4"):
+        seconds.landed(4)
     with scope("pass_columns"):
         p_gather.forward()
     with scope("wait_slab_rest"):
@@ -752,9 +754,10 @@
         def _(block):
             db[block] = left(block)
 
-    with scope("pass_second_factor"):
-        g_gather.forward(then=lambda number, index: g_to_sibling(number, index).start())
-
+    with scope("pass_seconds"):
+        seconds.passed(*EVENTS)
+    with scope("arrived_seconds"):
+        seconds.arrived(*EVENTS)
     with scope("finish_columns"):
         p_gather.finish()
 
@@ -814,10 +817,10 @@
     def start(copy):
         copy.start()
 
-    with scope("finish_second_factor"):
-        g_gather.finish(then=lambda number, index: g_to_sibling(number, index).start())
-        for number, index in ((3, y), (0, g_gather.down), (1, g_gather.up), (2, g_gather.far)):
-            g_from_sibling(number, index).wait_recv()
+    with scope("seconds_core"):
+        for number in range(4):
+            for block in range(3):
+                seconds.wait_core(number, 2 * block + 2)
     with scope("right_update"):
         for turn in (2, 1, 3, 0):
             block = (z // 2 + turn) % 4
@@ -858,9 +861,8 @@
                 turn_z(block, distance, lambda copy: copy.wait_send(), lambda copy: copy.wait())
             for distance in (1, 2, 3):
                 turn_x(block, distance).wait_send()
-        for event in EVENTS:
-            sent(event)
-            g_spread.sent(event)
+        panels.sent()
+        seconds.sent()
 
         @pl.when(f_source)
         def _():
@@ -881,12 +883,10 @@
             def _():
                 ga_copy(panel).wait_send()
 
-        for gather in (fxx, fxy, gxx, gxy, f_gather, p_gather, g_gather):
+        for gather in (fxx, fxy, gxx, gxy, f_gather, p_gather):
             gather.drain()
         fx_to_sibling.wait_send()
         gx_to_sibling.wait_send()
-        for number, index in ((3, y), (0, g_gather.down), (1, g_gather.up), (2, g_gather.far)):
-            g_to_sibling(number, index).wait_send()
 
 
 def on_device(*arrays):
@@ -948,10 +948,10 @@
         dma((8,)),
         dma((8,)),
         dma((8,)),
-        dma((4,)),
-        dma((4,)),
-        dma((4,)),
-        dma((4,)),
+        dma((3, 4)),
+        dma((3, 4)),
+        dma((4, 3)),
+        dma((4, 3)),
         dma((4,)),
         dma((4,)),
         dma((4, 3)),

time: 130 us -> 121 us (0.931); the launches traced: 128 us -> 121 us
  Pallas kernels: 125 us -> 118 us
    pallas_call x1, Pallas kernels: 125 us -> 118 us  [on_device(): pl.pallas_call(kernel, out_shape=jax.ShapeDtypeStruct((1536, 256), F32),...]
where the time goes in v3:
time: 121 us
  Pallas kernels  118 us (98%)
  local copies, waits for them, and re-layouts  2.65 us (2%)
    pallas_call x1, Pallas kernels, on_device(): pl.pallas_call(kernel, out_shape=jax.ShapeDtypeStruct((1536, 256), F32),...  118 us
    unnamed x1, local copies, waits for them, and re-layouts  2.65 us

profile of v3, /device:TPU:1, one launch (start us, length us, event | category | flops | bytes accessed | tf_op | source)
XLA Modules:
  0.0 120.9 jit_solution(4289992289521195834)
XLA Ops:
  0.0 118.2 %two_sided_panels.1 = f32[1536,256]{1,0:T(8,128)} custom-call(f32[1536,256]{1,0:T(8,128)} %slab.1, f32[2,512,512]{2,1,0:T(8,128)} %inverse1.1, f32[2,32,1536]{2,1,0:T(8,128)} %factor1.1, f32[2,512,512]{2,1,0:T(8,128)} %inverse2.1, f32[2,32,256]{2,1,0:T(8,128)} %factor2.1), custom_call_target="tpu_custom_call" | custom-call | tf_op jit(solution)/shard_map/two_sided_panels/pallas_call | solution.py:962
  118.2 2.7 %copy.7 = f32[1536,256]{1,0:T(8,128)} copy(f32[1536,256]{1,0:T(8,128)} %two_sided_panels.1) | data formatting | bytes 3145728

commit v4 on v3

--- a/solution.py
+++ b/solution.py
@@ -730,6 +730,8 @@
 
     with scope("seconds_4"):
         seconds.landed(4)
+    with scope("pass_seconds_0"):
+        seconds.passed(0, 1, -1)
     with scope("pass_columns"):
         p_gather.forward()
     with scope("wait_slab_rest"):
@@ -748,6 +750,8 @@
             for block in range(1, 4):
                 xt[block, pl.ds(0, 128)] = jnp.zeros((128, 256), F32)
 
+    with scope("pass_seconds"):
+        seconds.passed(2, -2)
     with scope("left_update_rest"):
 
         @pl.loop(1, 4)
@@ -755,7 +759,7 @@
             db[block] = left(block)
 
     with scope("pass_seconds"):
-        seconds.passed(*EVENTS)
+        seconds.passed(3, -3, 4)
     with scope("arrived_seconds"):
         seconds.arrived(*EVENTS)
     with scope("finish_columns"):

time: 121 us -> 119 us (0.983)
    pallas_call x1, Pallas kernels: 118 us -> 117 us  [on_device(): pl.pallas_call(kernel, out_shape=jax.ShapeDtypeStruct((1536, 256), F32),...]
where the time goes in v4:
time: 119 us
  Pallas kernels  117 us (98%)
  local copies, waits for them, and re-layouts  2.65 us (2%)
    pallas_call x1, Pallas kernels, on_device(): pl.pallas_call(kernel, out_shape=jax.ShapeDtypeStruct((1536, 256), F32),...  117 us
    unnamed x1, local copies, waits for them, and re-layouts  2.65 us

profile of v4, /device:TPU:1, one launch (start us, length us, event | category | flops | bytes accessed | tf_op | source)
XLA Modules:
  0.0 119.3 jit_solution(16171953827054735437)
XLA Ops:
  0.0 116.6 %two_sided_panels.1 = f32[1536,256]{1,0:T(8,128)} custom-call(f32[1536,256]{1,0:T(8,128)} %slab.1, f32[2,512,512]{2,1,0:T(8,128)} %inverse1.1, f32[2,32,1536]{2,1,0:T(8,128)} %factor1.1, f32[2,512,512]{2,1,0:T(8,128)} %inverse2.1, f32[2,32,256]{2,1,0:T(8,128)} %factor2.1), custom_call_target="tpu_custom_call" | custom-call | tf_op jit(solution)/shard_map/two_sided_panels/pallas_call | solution.py:966
  116.6 2.7 %copy.7 = f32[1536,256]{1,0:T(8,128)} copy(f32[1536,256]{1,0:T(8,128)} %two_sided_panels.1) | data formatting | bytes 3145728

commit v5 on v4

--- a/solution.py
+++ b/solution.py
@@ -760,8 +760,6 @@
 
     with scope("pass_seconds"):
         seconds.passed(3, -3, 4)
-    with scope("arrived_seconds"):
-        seconds.arrived(*EVENTS)
     with scope("finish_columns"):
         p_gather.finish()
 
@@ -821,6 +819,8 @@
     def start(copy):
         copy.start()
 
+    with scope("arrived_seconds"):
+        seconds.arrived(*EVENTS)
     with scope("seconds_core"):
         for number in range(4):
             for block in range(3):

time: 119 us -> 120 us (level)
  no operation moved by 1% of the time
where the time goes in v5:
time: 120 us
  Pallas kernels  118 us (98%)
  local copies, waits for them, and re-layouts  2.65 us (2%)
    pallas_call x1, Pallas kernels, on_device(): pl.pallas_call(kernel, out_shape=jax.ShapeDtypeStruct((1536, 256), F32),...  118 us
    unnamed x1, local copies, waits for them, and re-layouts  2.65 us

profile of v5, /device:TPU:1, one launch (start us, length us, event | category | flops | bytes accessed | tf_op | source)
XLA Modules:
  0.0 120.3 jit_solution(6828901102311841924)
XLA Ops:
  0.0 117.6 %two_sided_panels.1 = f32[1536,256]{1,0:T(8,128)} custom-call(f32[1536,256]{1,0:T(8,128)} %slab.1, f32[2,512,512]{2,1,0:T(8,128)} %inverse1.1, f32[2,32,1536]{2,1,0:T(8,128)} %factor1.1, f32[2,512,512]{2,1,0:T(8,128)} %inverse2.1, f32[2,32,256]{2,1,0:T(8,128)} %factor2.1), custom_call_target="tpu_custom_call" | custom-call | tf_op jit(solution)/shard_map/two_sided_panels/pallas_call | solution.py:966
  117.6 2.7 %copy.7 = f32[1536,256]{1,0:T(8,128)} copy(f32[1536,256]{1,0:T(8,128)} %two_sided_panels.1) | data formatting | bytes 3145728
